TPU v7x, 512 devices: a whole 4x4x16 slice. The times are simulated.
512 devices in a mesh: tok: 128 (over y, z, core), head: 4 (over x).
Axes of the slice: x: 4, y: 4, z: 16, core: 2. Of those that a mesh axis runs over, the one named last changes fastest.
Arguments:
- queries: bfloat16 [4, 32768, 256], P('head', 'tok'), may hold values from -5 to 5
- key_vectors: bfloat16 [4, 32768, 256], P('head', 'tok'), may hold values from -5 to 5
- value_vectors: bfloat16 [4, 32768, 256], P('head', 'tok'), may hold values from -8 to 8
- token_rate: float32 [4, 32768], P('head', 'tok'), may hold values from 0.1 to 1
- fast_gate: bfloat16 [4, 512, 256], P('head'), may hold values from -0.375 to 0.375
- fast_up: bfloat16 [4, 512, 256], P('head'), may hold values from -0.375 to 0.375
- fast_down: bfloat16 [4, 512, 256], P('head'), may hold values from -0.25 to 0.25
- attention_gain: float32 [4, 256], P('head'), may hold values from 0.25 to 1.75
- memory_gain: float32 [4, 256], P('head'), may hold values from 0.25 to 1.75
Outputs:
- layer_output: bfloat16 [4, 32768, 256], P('head', 'tok')
All inputs are finite; a program needn't handle non-finite values.
Results may differ from a plain program's by a relative error of at most 0.0065.
Values may be sent and summed in bfloat16 or wider, within the bound.
No kernel may reach another device: no remote copies, remote signals or barrier semaphores. Data moves between devices by JAX's collectives and lax.ppermute only.
A program may use at most 64 MiB of HBM per device.

v0:
```python
import jax
import jax.numpy as jnp
from jax import lax
from jax.sharding import Mesh
from jax.sharding import PartitionSpec as P

BLOCK = 256
HALO = 128
NS_STEPS = 2
TOK = ("y", "zh", "zl", "c")
NEAR = ("y", "zl")
FAR = "zh"
PAIR = "c"
first_coeff = 3.4445
second_coeff = -4.775
third_coefficient = 2.0315
step_size = 1.0
norm_floor = 1e-07
epsilon = 1e-06
masked_score = -1e30


def dot(a, b, dims, precision=None):
    return lax.dot_general(
        a, b, (dims, ((), ())), precision=precision, preferred_element_type=jnp.float32
    )


def outer_halo(keys, values, core):
    count = lax.axis_size(TOK)
    swap = [(i, i + 1) for i in range(1, count - 1, 2)] + [
        (i + 1, i) for i in range(1, count - 1, 2)
    ]
    stacked = jnp.stack([keys, values])
    edge = jnp.where(core == 0, stacked[:, :HALO], stacked[:, -HALO:])
    return lax.ppermute(edge, TOK, swap)


def copies_to(array, axis):
    copies = jnp.broadcast_to(array, (lax.axis_size(axis), *array.shape))
    return lax.all_to_all(copies, axis, split_axis=0, concat_axis=0, tiled=True)


def window_attention(queries, pair_keys, pair_values, outer, core, has_outer):
    head_depth = queries.shape[1]
    start = core * HALO
    width = 2 * BLOCK - HALO
    keys = lax.dynamic_slice_in_dim(pair_keys, start, width, 0)
    values = lax.dynamic_slice_in_dim(pair_values, start, width, 0)
    scale = head_depth ** (-0.5)
    inner = dot(queries, keys, ((1,), (1,))) * scale
    outside = dot(queries, outer[0], ((1,), (1,))) * scale
    outside = jnp.where(has_outer, outside, masked_score)
    highest = jnp.maximum(
        jnp.max(inner, axis=1, keepdims=True), jnp.max(outside, axis=1, keepdims=True)
    )
    inner = jnp.exp(inner - highest)
    outside = jnp.exp(outside - highest)
    total = jnp.sum(inner, axis=1, keepdims=True) + jnp.sum(outside, axis=1, keepdims=True)
    inner = (inner / total).astype(jnp.bfloat16)
    outside = (outside / total).astype(jnp.bfloat16)
    return dot(inner, values, ((1,), (0,))) + dot(outside, outer[1], ((1,), (0,)))


def fast_gradients(keys, scaled, gate_weights, up_weights, down_weights):
    gate_value = dot(keys, gate_weights, ((1,), (1,)))
    up_value = dot(keys, up_weights, ((1,), (1,)))
    squashed = jax.nn.sigmoid(gate_value)
    hidden = (gate_value * squashed * up_value).astype(jnp.bfloat16)
    backward = dot(scaled, down_weights, ((1,), (1,)))
    gate_grad = (backward * up_value * squashed * (1.0 + gate_value * (1.0 - squashed))).astype(
        jnp.bfloat16
    )
    up_grad = (backward * gate_value * squashed).astype(jnp.bfloat16)
    return jnp.concatenate(
        [
            dot(gate_grad, keys, ((0,), (0,))).astype(jnp.bfloat16),
            dot(up_grad, keys, ((0,), (0,))).astype(jnp.bfloat16),
            dot(hidden, scaled, ((0,), (0,))).astype(jnp.bfloat16),
        ],
        axis=1,
    )


def sum_over_tokens(grads):
    near = lax.axis_size(NEAR)
    tiles = grads.reshape(near, -1, grads.shape[1])
    arrived = lax.all_to_all(tiles, NEAR, split_axis=0, concat_axis=0, tiled=True)
    own = jnp.sum(arrived.astype(jnp.float32), axis=0).astype(jnp.bfloat16)
    own = jnp.sum(copies_to(own, FAR).astype(jnp.float32), axis=0).astype(jnp.bfloat16)
    half = copies_to(own, NEAR).reshape(grads.shape)
    return lax.all_gather(half, PAIR, axis=0, tiled=True)


def orthogonalize(grad):
    grad = grad.astype(jnp.float32)
    current = grad * (1.0 / (jnp.sqrt(jnp.sum(grad * grad)) + norm_floor))
    for iteration in range(NS_STEPS):
        product = dot(current, current, ((0,), (0,)), lax.Precision.HIGH)
        squared = dot(product, product, ((1,), (0,)), lax.Precision.HIGH)
        mixer = second_coeff * product + third_coefficient * squared
        current = first_coeff * current + dot(current, mixer, ((1,), (0,)), lax.Precision.HIGH)
    return current


def on_device(
    queries,
    key_vectors,
    value_vectors,
    token_rate,
    fast_gate,
    fast_up,
    fast_down,
    attention_gain,
    memory_gain,
):
    queries, keys, values = (queries[0], key_vectors[0], value_vectors[0])
    rates = token_rate[0]
    head_depth = queries.shape[1]
    hidden_units = fast_gate.shape[1]
    core = lax.axis_index(PAIR)
    index = lax.axis_index(TOK)
    has_outer = jnp.where(core == 0, index > 0, index < lax.axis_size(TOK) - 1)
    scaled = (rates[:, None] * values.astype(jnp.float32)).astype(jnp.bfloat16)
    pair = lax.all_gather(jnp.stack([keys, scaled, values]), PAIR, axis=1, tiled=True)
    half = hidden_units // 2
    mine = [
        lax.dynamic_slice_in_dim(w[0], core * half, half, 0)
        for w in (fast_gate, fast_up, fast_down)
    ]
    grads = fast_gradients(pair[0], pair[1], *mine)
    summed = sum_over_tokens(grads)
    outer = outer_halo(keys, values, core)
    attended = window_attention(queries, pair[0], pair[2], outer, core, has_outer)
    squares = jnp.sum(attended * attended, axis=1)
    width_sum = jnp.sum(copies_to(squares.reshape(1, -1), "head"), axis=0)[0]
    width_mean = width_sum / (lax.axis_size("head") * head_depth)
    attention_part = attended * lax.rsqrt(width_mean + epsilon)[:, None] * attention_gain
    renewed = []
    for i, w in enumerate((fast_gate, fast_up, fast_down)):
        update = orthogonalize(summed[:, i * head_depth : (i + 1) * head_depth])
        renewed.append((w[0].astype(jnp.float32) + step_size * update).astype(jnp.bfloat16))
    gate_value = dot(queries, renewed[0], ((1,), (1,)))
    up_value = dot(queries, renewed[1], ((1,), (1,)))
    memory_hidden = (jax.nn.silu(gate_value) * up_value).astype(jnp.bfloat16)
    memory = dot(memory_hidden, renewed[2], ((1,), (0,)))
    memory_mean = jnp.mean(memory * memory, axis=1, keepdims=True)
    memory_part = memory * lax.rsqrt(memory_mean + epsilon) * memory_gain
    return (attention_part + memory_part).astype(jnp.bfloat16)[None]


def solution(mesh):
    finer = Mesh(
        mesh.devices.reshape(4, 4, 4, 2, mesh.shape["head"]), ("y", "zh", "zl", "c", "head")
    )
    return jax.shard_map(
        on_device,
        mesh=finer,
        in_specs=(
            P("head", TOK, None),
            P("head", TOK, None),
            P("head", TOK, None),
            P("head", TOK),
            P("head", None, None),
            P("head", None, None),
            P("head", None, None),
            P("head", None),
            P("head", None),
        ),
        out_specs=P("head", TOK, None),
        check_vma=False,
    )
```

profile of v0, /device:TPU:1, one launch (start us, length us, event | category | flops | bytes accessed | tf_op | source)
XLA Modules:
  0.0 101.0 jit_solution(8072750087071840205)
XLA Ops:
  0.0 0.0 copy-start
  0.0 0.7 copy-done.6
  0.7 1.1 %multiply_convert_fusion.3 = bf16[1,256,256]{2,1,0:T(8,128)(2,1)S(1)} fusion(bf16[1,256,256]{2,1,0:T(8,128)(2,1)} %param.11, f32[256]{0:T(256)S(1)} %bitcast.115), kind=kLoop, calls=%fused_computation.82 | loop fusion | flops 196608 | bytes 263168 | tf_op jit(solution)/shard_map/convert_element_type | solution.py:124
  1.8 0.0 copy-done.1
  1.8 0.0 copy-done.5
  1.9 0.0 copy-start.2
  1.9 9.0 %all_gather.6 = bf16[3,512,256]{2,1,0:T(8,128)(2,1)S(1)} all-gather(bf16[3,256,256]{2,1,0:T(8,128)(2,1)S(1)} %pad_maximum_fusion), channel_id=1, replica_groups=mesh['y'=4,'zh'=4,'zl'=4,'c'=2,'head'=4] {'c'}, dimensions={1}, use_global_device_ids=true | all-gather | bytes 1179648 | tf_op jit(solution)/shard_map/all_gather | solution.py:125
  10.9 0.0 copy-done.2
  10.9 0.3 fusion.33
  11.1 0.7 copy-done.3
  11.8 0.3 fusion.35
  12.1 0.7 copy-done.4
  12.8 0.3 fusion.44
  13.0 0.4 convolution_convert_fusion.1
  13.4 0.4 convolution_convert_fusion.2
  13.8 0.4 convolution_convert_fusion
  14.2 0.9 copy.16
  15.2 3.6 %all-to-all-start.1 = ((bf16[16,16,768]{2,1,0:T(8,128)(2,1)}), bf16[16,16,768]{2,1,0:T(8,128)(2,1)S(1)}, u32[]{:S(2)}, u32[]{:S(2)}) async-start(bf16[16,16,768]{2,1,0:T(8,128)(2,1)} %bitcast.13), calls=%async_computation.1 | async-start | bytes 786432 | tf_op jit(solution)/shard_map/all_to_all | solution.py:88
  18.8 3.7 %collective-permute-start = (bf16[2,128,256]{2,1,0:T(8,128)(2,1)S(1)}, bf16[2,128,256]{2,1,0:T(8,128)(2,1)S(1)}, u32[]{:S(2)}, u32[]{:S(2)}) collective-permute-start(bf16[2,128,256]{2,1,0:T(8,128)(2,1)S(1)} %slice_select_fusion), channel_id=1, source_target_pairs={{4,8},{12,16},{20,24},{28,32},{36,40},{44,48},{52,56},{60,64},{68,... | collective-permute-start | bytes 393224 | tf_op jit(solution)/shard_map/ppermute | solution.py:36
  22.6 0.3 fusion.86
  22.8 5.5 %collective-permute-done = bf16[2,128,256]{2,1,0:T(8,128)(2,1)S(1)} collective-permute-done((bf16[2,128,256]{2,1,0:T(8,128)(2,1)S(1)}, bf16[2,128,256]{2,1,0:T(8,128)(2,1)S(1)}, u32[]{:S(2)}, u32[]{:S(2)}) %collective-permute-start) | collective-permute-done | bytes 131104 | tf_op jit(solution)/shard_map/ppermute | solution.py:36
  28.3 0.2 fusion.87
  28.6 0.1 fusion.30
  28.7 3.1 %all-to-all-done.1 = bf16[16,16,768]{2,1,0:T(8,128)(2,1)S(1)} async-done(((bf16[16,16,768]{2,1,0:T(8,128)(2,1)}), bf16[16,16,768]{2,1,0:T(8,128)(2,1)S(1)}, u32[]{:S(2)}, u32[]{:S(2)}) %all-to-all-start.1) | async-done | bytes 393248 | tf_op jit(solution)/shard_map/all_to_all | solution.py:88
  31.8 0.1 reduce_sum.100
  31.8 0.6 broadcast_in_dim.24
  32.5 11.5 %all-to-all-start.2 = ((bf16[4,16,768]{2,1,0:T(8,128)(2,1)}), bf16[4,16,768]{2,1,0:T(8,128)(2,1)S(1)}, u32[]{:S(2)}, u32[]{:S(2)}) async-start(bf16[4,16,768]{2,1,0:T(8,128)(2,1)} %broadcast_in_dim.24), calls=%async_computation.2 | async-start | bytes 196608 | tf_op jit(solution)/shard_map/all_to_all | solution.py:41
  44.0 0.3 fusion.51
  44.3 0.3 multiply_reduce_fusion.1
  44.5 11.4 %all-to-all-done.2 = bf16[4,16,768]{2,1,0:T(8,128)(2,1)S(1)} async-done(((bf16[4,16,768]{2,1,0:T(8,128)(2,1)}), bf16[4,16,768]{2,1,0:T(8,128)(2,1)S(1)}, u32[]{:S(2)}, u32[]{:S(2)}) %all-to-all-start.2) | async-done | bytes 98336 | tf_op jit(solution)/shard_map/all_to_all | solution.py:41
  55.9 0.6 broadcast_in_dim.23
  56.5 4.0 %all-to-all-start = ((f32[4,1,256]{2,1,0:T(1,128)}), f32[4,1,256]{2,1,0:T(1,128)S(1)}, u32[]{:S(2)}, u32[]{:S(2)}) async-start(f32[4,1,256]{2,1,0:T(1,128)} %broadcast_in_dim.23), calls=%async_computation | async-start | bytes 8192 | tf_op jit(solution)/shard_map/all_to_all | solution.py:41
  60.6 4.1 %all-to-all-done = f32[4,1,256]{2,1,0:T(1,128)S(1)} async-done(((f32[4,1,256]{2,1,0:T(1,128)}), f32[4,1,256]{2,1,0:T(1,128)S(1)}, u32[]{:S(2)}, u32[]{:S(2)}) %all-to-all-start) | async-done | bytes 4128 | tf_op jit(solution)/shard_map/all_to_all | solution.py:41
  64.7 0.8 broadcast_in_dim.25
  65.4 5.1 %all-to-all-start.3 = ((bf16[16,16,768]{2,1,0:T(8,128)(2,1)}), bf16[16,16,768]{2,1,0:T(8,128)(2,1)S(1)}, u32[]{:S(2)}, u32[]{:S(2)}) async-start(bf16[16,16,768]{2,1,0:T(8,128)(2,1)} %broadcast_in_dim.25), calls=%async_computation.3 | async-start | bytes 786432 | tf_op jit(solution)/shard_map/all_to_all | solution.py:41
  70.6 9.9 %all-to-all-done.3 = bf16[16,16,768]{2,1,0:T(8,128)(2,1)S(1)} async-done(((bf16[16,16,768]{2,1,0:T(8,128)(2,1)}), bf16[16,16,768]{2,1,0:T(8,128)(2,1)S(1)}, u32[]{:S(2)}, u32[]{:S(2)}) %all-to-all-start.3) | async-done | bytes 393248 | tf_op jit(solution)/shard_map/all_to_all | solution.py:41
  80.5 7.4 %all_gather.7 = bf16[512,768]{1,0:T(8,128)(2,1)S(1)} all-gather(bf16[256,768]{1,0:T(8,128)(2,1)S(1)} %bitcast.114), channel_id=1, replica_groups=mesh['y'=4,'zh'=4,'zl'=4,'c'=2,'head'=4] {'c'}, dimensions={0}, use_global_device_ids=true | all-gather | bytes 1179648 | tf_op jit(solution)/shard_map/all_gather | solution.py:92
  87.9 0.8 fusion.22
  89.5 0.6 fusion.20
  90.1 0.3 fusion.13
  90.4 0.4 convolution_add_fusion.5
  90.7 0.6 fusion.90
  91.4 0.3 fusion.12
  91.6 0.4 fusion.4
  92.0 0.2 convolution_bitcast_fusion.1
  93.0 0.6 fusion.18
  93.6 0.3 fusion.11
  93.8 0.4 convolution_add_fusion.3
  94.2 0.6 fusion.91
  94.8 0.3 fusion.10
  95.1 0.4 fusion.5
  96.3 0.6 fusion.16
  96.9 0.3 fusion.9
  97.2 0.4 convolution_add_fusion.1
  97.6 0.6 fusion.92
  98.2 0.3 fusion.8
  98.5 0.4 fusion.6
  98.9 0.0 copy-start.8
  98.9 0.5 multiply_reduce_fusion
  99.4 0.0 copy-start.7
  99.4 0.1 copy-done.8
  99.6 0.5 copy-done.7
  100.1 0.1 fusion.57
  100.2 0.8 copy.17
  (19 shorter events, 0.3 us)
Async XLA Ops:
  0.0 22.6 %copy-start = (bf16[1,256,256]{2,1,0:T(8,128)(2,1)S(1)}, bf16[1,256,256]{2,1,0:T(8,128)(2,1)}, u32[]{:S(2)}) copy-start(bf16[1,256,256]{2,1,0:T(8,128)(2,1)} %param.9) | copy-start | bytes 393220
  0.0 0.7 copy-start.6
  0.7 1.1 %copy-start.1 = (bf16[1,256,256]{2,1,0:T(8,128)(2,1)S(1)}, bf16[1,256,256]{2,1,0:T(8,128)(2,1)}, u32[]{:S(2)}) copy-start(bf16[1,256,256]{2,1,0:T(8,128)(2,1)} %param.11) | copy-start | bytes 393220
  0.7 1.1 %copy-start.5 = (bf16[1,256,256]{2,1,0:T(8,128)(2,1)S(1)}, bf16[1,256,256]{2,1,0:T(8,128)(2,1)}, u32[]{:S(2)}) copy-start(bf16[1,256,256]{2,1,0:T(8,128)(2,1)} %param.10) | copy-start | bytes 393220
  1.9 9.0 %copy-start.2 = (bf16[1,512,256]{2,1,0:T(8,128)(2,1)S(1)}, bf16[1,512,256]{2,1,0:T(8,128)(2,1)}, u32[]{:S(2)}) copy-start(bf16[1,512,256]{2,1,0:T(8,128)(2,1)} %param.13) | copy-start | bytes 786436
  10.9 1.0 copy-start.3
  11.8 0.9 copy-start.4
  15.2 16.6 %all-to-all-start.1 = ((bf16[16,16,768]{2,1,0:T(8,128)(2,1)}), bf16[16,16,768]{2,1,0:T(8,128)(2,1)S(1)}, u32[]{:S(2)}, u32[]{:S(2)}) async-start(bf16[16,16,768]{2,1,0:T(8,128)(2,1)} %bitcast.13), calls=%async_computation.1 | async-start | bytes 786432 | tf_op jit(solution)/shard_map/all_to_all | solution.py:88
  18.8 9.6 %collective-permute-start = (bf16[2,128,256]{2,1,0:T(8,128)(2,1)S(1)}, bf16[2,128,256]{2,1,0:T(8,128)(2,1)S(1)}, u32[]{:S(2)}, u32[]{:S(2)}) collective-permute-start(bf16[2,128,256]{2,1,0:T(8,128)(2,1)S(1)} %slice_select_fusion), channel_id=1, source_target_pairs={{4,8},{12,16},{20,24},{28,32},{36,40},{44,48},{52,56},{60,64},{68,... | collective-permute-start | bytes 393224 | tf_op jit(solution)/shard_map/ppermute | solution.py:36
  32.5 23.4 %all-to-all-start.2 = ((bf16[4,16,768]{2,1,0:T(8,128)(2,1)}), bf16[4,16,768]{2,1,0:T(8,128)(2,1)S(1)}, u32[]{:S(2)}, u32[]{:S(2)}) async-start(bf16[4,16,768]{2,1,0:T(8,128)(2,1)} %broadcast_in_dim.24), calls=%async_computation.2 | async-start | bytes 196608 | tf_op jit(solution)/shard_map/all_to_all | solution.py:41
  56.5 8.2 %all-to-all-start = ((f32[4,1,256]{2,1,0:T(1,128)}), f32[4,1,256]{2,1,0:T(1,128)S(1)}, u32[]{:S(2)}, u32[]{:S(2)}) async-start(f32[4,1,256]{2,1,0:T(1,128)} %broadcast_in_dim.23), calls=%async_computation | async-start | bytes 8192 | tf_op jit(solution)/shard_map/all_to_all | solution.py:41
  65.4 15.0 %all-to-all-start.3 = ((bf16[16,16,768]{2,1,0:T(8,128)(2,1)}), bf16[16,16,768]{2,1,0:T(8,128)(2,1)S(1)}, u32[]{:S(2)}, u32[]{:S(2)}) async-start(bf16[16,16,768]{2,1,0:T(8,128)(2,1)} %broadcast_in_dim.25), calls=%async_computation.3 | async-start | bytes 786432 | tf_op jit(solution)/shard_map/all_to_all | solution.py:41
  98.9 0.7 copy-start.8
  99.4 0.7 copy-start.7
where the time goes:
time: 102 us; the launch traced here: 101 us
  waiting for transfers between devices  34 us (33%)
  starting transfers between devices  27.8 us (27%)
  blocking collectives  16.4 us (16%)
  matrix products  11.4 us (11%)
  local copies, waits for them, and re-layouts  6.51 us (6%)
  between operations  2.55 us (2%)
  other arithmetic  2.41 us (2%)
    all_to_all x3, waiting for transfers between devices, copies_to(): return lax.all_to_all(copies, axis, split_axis=0, concat_axis=0, tiled=True)  25.4 us
    all_to_all x3, starting transfers between devices, copies_to(): return lax.all_to_all(copies, axis, split_axis=0, concat_axis=0, tiled=True)  20.6 us
    dot_general x30, matrix products, dot(): lax.dot_general(a, b, (dims, ((), ())), precision=precision, preferred_el...  11.4 us
    all_gather x1, blocking collectives, on_device(): lax.all_gather(jnp.stack([keys, scaled, values]), PAIR, axis=1, tiled=True)  8.97 us
    all_gather x1, blocking collectives, sum_over_tokens(): return lax.all_gather(half, PAIR, axis=0, tiled=True)  7.42 us
    ppermute x1, waiting for transfers between devices, outer_halo(): return lax.ppermute(edge, TOK, swap)  5.51 us
    ppermute x1, starting transfers between devices, outer_halo(): return lax.ppermute(edge, TOK, swap)  3.7 us
    all_to_all x1, starting transfers between devices, sum_over_tokens(): lax.all_to_all(tiles, NEAR, split_axis=0, concat_axis=0, tiled=True)  3.55 us
  transfers between devices with their start and end apart: 5, of which 5 were waited for; matrix products, arithmetic and copies ran while one was open for 1% of the time, Pallas kernels for 0%

commit v1 on v0

--- a/solution.py
+++ b/solution.py
@@ -122,7 +122,9 @@
     index = lax.axis_index(TOK)
     has_outer = jnp.where(core == 0, index > 0, index < lax.axis_size(TOK) - 1)
     scaled = (rates[:, None] * values.astype(jnp.float32)).astype(jnp.bfloat16)
-    pair = lax.all_gather(jnp.stack([keys, scaled, values]), PAIR, axis=1, tiled=True)
+    own_2 = jnp.stack([keys, scaled, values])
+    repeated = jnp.stack([own_2] * lax.axis_size(PAIR))
+    pair = jnp.concatenate(lax.all_to_all(repeated, PAIR, 0, 0), axis=1)
     half = hidden_units // 2
     mine = [
         lax.dynamic_slice_in_dim(w[0], core * half, half, 0)

time: 102 us -> 107 us (1.049)
  starting transfers between devices: 27.8 us -> 38.1 us
  blocking collectives: 16.4 us -> 7.42 us
  waiting for transfers between devices: 34 us -> 35.6 us
    all_to_all x0 -> x1, starting transfers between devices: none -> 10.4 us  [on_device(): pair = jnp.concatenate(lax.all_to_all(repeated, PAIR, 0, 0), axis=1)]
    all_gather x1 -> x0, blocking collectives: 8.97 us -> none  [on_device(): lax.all_gather(jnp.stack([keys, scaled, values]), PAIR, axis=1, tiled=True)]
    all_to_all x0 -> x1, waiting for transfers between devices: none -> 1.56 us  [on_device(): pair = jnp.concatenate(lax.all_to_all(repeated, PAIR, 0, 0), axis=1)]
  transfers between devices with their start and end apart: 5 -> 6, of which waited for: 5 -> 6; matrix products, arithmetic and copies ran while one was open for 1% -> 1% of each run, Pallas kernels for 0% -> 0%
where the time goes in v1:
time: 107 us; the launch traced here: 106 us
  starting transfers between devices  38.1 us (36%)
  waiting for transfers between devices  35.6 us (33%)
  matrix products  11.4 us (11%)
  local copies, waits for them, and re-layouts  7.43 us (7%)
  blocking collectives  7.42 us (7%)
  other arithmetic  3.34 us (3%)
  between operations  2.52 us (2%)
    all_to_all x3, waiting for transfers between devices, copies_to(): return lax.all_to_all(copies, axis, split_axis=0, concat_axis=0, tiled=True)  25.4 us
    all_to_all x3, starting transfers between devices, copies_to(): return lax.all_to_all(copies, axis, split_axis=0, concat_axis=0, tiled=True)  20.5 us
    dot_general x30, matrix products, dot(): lax.dot_general(a, b, (dims, ((), ())), precision=precision, preferred_el...  11.4 us
    all_to_all x1, starting transfers between devices, on_device(): pair = jnp.concatenate(lax.all_to_all(repeated, PAIR, 0, 0), axis=1)  10.4 us
    all_gather x1, blocking collectives, sum_over_tokens(): return lax.all_gather(half, PAIR, axis=0, tiled=True)  7.42 us
    ppermute x1, waiting for transfers between devices, outer_halo(): return lax.ppermute(edge, TOK, swap)  5.58 us
    unnamed x19, local copies, waits for them, and re-layouts  3.69 us
    ppermute x1, starting transfers between devices, outer_halo(): return lax.ppermute(edge, TOK, swap)  3.67 us
  transfers between devices with their start and end apart: 6, of which 6 were waited for; matrix products, arithmetic and copies ran while one was open for 1% of the time, Pallas kernels for 0%

profile of v1, /device:TPU:1, one launch (start us, length us, event | category | flops | bytes accessed | tf_op | source)
XLA Modules:
  0.0 105.8 jit_solution(6411292059007035951)
XLA Ops:
  0.0 0.7 copy-done.6
  0.7 1.1 %multiply_convert_fusion.3 = bf16[1,256,256]{2,1,0:T(8,128)(2,1)S(1)} fusion(bf16[1,256,256]{2,1,0:T(8,128)(2,1)} %param.11, f32[256]{0:T(256)S(1)} %bitcast.115), kind=kLoop, calls=%fused_computation.76 | loop fusion | flops 196608 | bytes 263168 | tf_op jit(solution)/shard_map/convert_element_type | solution.py:124
  1.9 0.9 pad_maximum_fusion
  2.8 10.4 %all-to-all-start = ((bf16[2,3,256,256]{3,2,1,0:T(8,128)(2,1)}), bf16[2,3,256,256]{3,2,1,0:T(8,128)(2,1)S(1)}, u32[]{:S(2)}, u32[]{:S(2)}) async-start(bf16[2,3,256,256]{3,2,1,0:T(8,128)(2,1)} %pad_maximum_fusion), calls=%async_computation | async-start | bytes 1572864 | tf_op jit(solution)/shard_map/all_to_all | solution.py:127
  13.2 1.6 %all-to-all-done = bf16[2,3,256,256]{3,2,1,0:T(8,128)(2,1)S(1)} async-done(((bf16[2,3,256,256]{3,2,1,0:T(8,128)(2,1)}), bf16[2,3,256,256]{3,2,1,0:T(8,128)(2,1)S(1)}, u32[]{:S(2)}, u32[]{:S(2)}) %all-to-all-start) | async-done | bytes 786464 | tf_op jit(solution)/shard_map/all_to_all | solution.py:127
  14.7 0.1 fusion.75
  14.8 0.9 copy-done.2
  15.7 0.3 fusion.49
  15.9 0.7 copy-done.4
  16.6 0.3 fusion.51
  16.9 0.7 copy-done.3
  17.6 0.3 fusion.53
  17.9 0.4 convolution_convert_fusion.1
  18.2 0.4 convolution_convert_fusion.2
  18.7 0.4 convolution_convert_fusion
  19.1 0.9 copy.16
  20.0 3.6 %all-to-all-start.2 = ((bf16[16,16,768]{2,1,0:T(8,128)(2,1)}), bf16[16,16,768]{2,1,0:T(8,128)(2,1)S(1)}, u32[]{:S(2)}, u32[]{:S(2)}) async-start(bf16[16,16,768]{2,1,0:T(8,128)(2,1)} %bitcast.14), calls=%async_computation.2 | async-start | bytes 786432 | tf_op jit(solution)/shard_map/all_to_all | solution.py:88
  23.6 3.7 %collective-permute-start = (bf16[2,128,256]{2,1,0:T(8,128)(2,1)S(1)}, bf16[2,128,256]{2,1,0:T(8,128)(2,1)S(1)}, u32[]{:S(2)}, u32[]{:S(2)}) collective-permute-start(bf16[2,128,256]{2,1,0:T(8,128)(2,1)S(1)} %slice_select_fusion), channel_id=1, source_target_pairs={{4,8},{12,16},{20,24},{28,32},{36,40},{44,48},{52,56},{60,64},{68,... | collective-permute-start | bytes 393224 | tf_op jit(solution)/shard_map/ppermute | solution.py:36
  27.3 0.0 copy-done
  27.3 0.3 fusion.76
  27.6 5.6 %collective-permute-done = bf16[2,128,256]{2,1,0:T(8,128)(2,1)S(1)} collective-permute-done((bf16[2,128,256]{2,1,0:T(8,128)(2,1)S(1)}, bf16[2,128,256]{2,1,0:T(8,128)(2,1)S(1)}, u32[]{:S(2)}, u32[]{:S(2)}) %collective-permute-start) | collective-permute-done | bytes 131104 | tf_op jit(solution)/shard_map/ppermute | solution.py:36
  33.2 0.2 fusion.77
  33.5 0.1 fusion.30
  33.6 3.1 %all-to-all-done.2 = bf16[16,16,768]{2,1,0:T(8,128)(2,1)S(1)} async-done(((bf16[16,16,768]{2,1,0:T(8,128)(2,1)}), bf16[16,16,768]{2,1,0:T(8,128)(2,1)S(1)}, u32[]{:S(2)}, u32[]{:S(2)}) %all-to-all-start.2) | async-done | bytes 393248 | tf_op jit(solution)/shard_map/all_to_all | solution.py:88
  36.7 0.1 reduce_sum.100
  36.7 0.6 broadcast_in_dim.24
  37.4 11.4 %all-to-all-start.3 = ((bf16[4,16,768]{2,1,0:T(8,128)(2,1)}), bf16[4,16,768]{2,1,0:T(8,128)(2,1)S(1)}, u32[]{:S(2)}, u32[]{:S(2)}) async-start(bf16[4,16,768]{2,1,0:T(8,128)(2,1)} %broadcast_in_dim.24), calls=%async_computation.3 | async-start | bytes 196608 | tf_op jit(solution)/shard_map/all_to_all | solution.py:41
  48.8 0.3 fusion.44
  49.1 0.3 multiply_reduce_fusion.1
  49.3 11.4 %all-to-all-done.3 = bf16[4,16,768]{2,1,0:T(8,128)(2,1)S(1)} async-done(((bf16[4,16,768]{2,1,0:T(8,128)(2,1)}), bf16[4,16,768]{2,1,0:T(8,128)(2,1)S(1)}, u32[]{:S(2)}, u32[]{:S(2)}) %all-to-all-start.3) | async-done | bytes 98336 | tf_op jit(solution)/shard_map/all_to_all | solution.py:41
  60.8 0.6 broadcast_in_dim.23
  61.4 4.0 %all-to-all-start.1 = ((f32[4,1,256]{2,1,0:T(1,128)}), f32[4,1,256]{2,1,0:T(1,128)S(1)}, u32[]{:S(2)}, u32[]{:S(2)}) async-start(f32[4,1,256]{2,1,0:T(1,128)} %broadcast_in_dim.23), calls=%async_computation.1 | async-start | bytes 8192 | tf_op jit(solution)/shard_map/all_to_all | solution.py:41
  65.4 4.1 %all-to-all-done.1 = f32[4,1,256]{2,1,0:T(1,128)S(1)} async-done(((f32[4,1,256]{2,1,0:T(1,128)}), f32[4,1,256]{2,1,0:T(1,128)S(1)}, u32[]{:S(2)}, u32[]{:S(2)}) %all-to-all-start.1) | async-done | bytes 4128 | tf_op jit(solution)/shard_map/all_to_all | solution.py:41
  69.5 0.8 broadcast_in_dim.25
  70.3 5.1 %all-to-all-start.4 = ((bf16[16,16,768]{2,1,0:T(8,128)(2,1)}), bf16[16,16,768]{2,1,0:T(8,128)(2,1)S(1)}, u32[]{:S(2)}, u32[]{:S(2)}) async-start(bf16[16,16,768]{2,1,0:T(8,128)(2,1)} %broadcast_in_dim.25), calls=%async_computation.4 | async-start | bytes 786432 | tf_op jit(solution)/shard_map/all_to_all | solution.py:41
  75.4 9.9 %all-to-all-done.4 = bf16[16,16,768]{2,1,0:T(8,128)(2,1)S(1)} async-done(((bf16[16,16,768]{2,1,0:T(8,128)(2,1)}), bf16[16,16,768]{2,1,0:T(8,128)(2,1)S(1)}, u32[]{:S(2)}, u32[]{:S(2)}) %all-to-all-start.4) | async-done | bytes 393248 | tf_op jit(solution)/shard_map/all_to_all | solution.py:41
  85.3 7.4 %all_gather.3 = bf16[512,768]{1,0:T(8,128)(2,1)S(1)} all-gather(bf16[256,768]{1,0:T(8,128)(2,1)S(1)} %bitcast.111), channel_id=1, replica_groups=mesh['y'=4,'zh'=4,'zl'=4,'c'=2,'head'=4] {'c'}, dimensions={0}, use_global_device_ids=true | all-gather | bytes 1179648 | tf_op jit(solution)/shard_map/all_gather | solution.py:92
  92.7 0.8 fusion.22
  95.7 0.6 fusion.20
  96.3 0.3 fusion.13
  96.6 0.4 convolution_add_fusion.5
  97.0 0.6 fusion.80
  97.6 0.3 fusion.12
  97.9 0.4 fusion.4
  98.3 0.3 convolution_bitcast_fusion.1
  98.6 0.6 fusion.16
  99.2 0.3 fusion.9
  99.4 0.4 convolution_add_fusion.1
  99.8 0.6 fusion.82
  100.5 0.3 fusion.8
  100.7 0.4 fusion.6
  101.1 0.6 fusion.18
  101.7 0.3 fusion.11
  102.0 0.4 convolution_add_fusion.3
  102.4 0.6 fusion.81
  103.0 0.3 fusion.10
  103.3 0.4 fusion.5
  103.7 0.0 copy-start.8
  103.7 0.5 multiply_reduce_fusion
  104.2 0.0 copy-start.7
  104.3 0.1 copy-done.8
  104.4 0.5 copy-done.7
  104.9 0.1 fusion.48
  105.1 0.8 copy.17
  (21 shorter events, 0.2 us)
Async XLA Ops:
  0.0 27.3 %copy-start = (bf16[1,256,256]{2,1,0:T(8,128)(2,1)S(1)}, bf16[1,256,256]{2,1,0:T(8,128)(2,1)}, u32[]{:S(2)}) copy-start(bf16[1,256,256]{2,1,0:T(8,128)(2,1)} %param.9) | copy-start | bytes 393220
  0.0 0.7 copy-start.6
  0.7 1.1 %copy-start.1 = (bf16[1,256,256]{2,1,0:T(8,128)(2,1)S(1)}, bf16[1,256,256]{2,1,0:T(8,128)(2,1)}, u32[]{:S(2)}) copy-start(bf16[1,256,256]{2,1,0:T(8,128)(2,1)} %param.11) | copy-start | bytes 393220
  0.7 1.1 %copy-start.5 = (bf16[1,256,256]{2,1,0:T(8,128)(2,1)S(1)}, bf16[1,256,256]{2,1,0:T(8,128)(2,1)}, u32[]{:S(2)}) copy-start(bf16[1,256,256]{2,1,0:T(8,128)(2,1)} %param.10) | copy-start | bytes 393220
  2.8 11.9 %all-to-all-start = ((bf16[2,3,256,256]{3,2,1,0:T(8,128)(2,1)}), bf16[2,3,256,256]{3,2,1,0:T(8,128)(2,1)S(1)}, u32[]{:S(2)}, u32[]{:S(2)}) async-start(bf16[2,3,256,256]{3,2,1,0:T(8,128)(2,1)} %pad_maximum_fusion), calls=%async_computation | async-start | bytes 1572864 | tf_op jit(solution)/shard_map/all_to_all | solution.py:127
  14.7 0.9 copy-start.2
  15.7 0.9 copy-start.4
  16.6 0.9 copy-start.3
  20.0 16.7 %all-to-all-start.2 = ((bf16[16,16,768]{2,1,0:T(8,128)(2,1)}), bf16[16,16,768]{2,1,0:T(8,128)(2,1)S(1)}, u32[]{:S(2)}, u32[]{:S(2)}) async-start(bf16[16,16,768]{2,1,0:T(8,128)(2,1)} %bitcast.14), calls=%async_computation.2 | async-start | bytes 786432 | tf_op jit(solution)/shard_map/all_to_all | solution.py:88
  23.6 9.6 %collective-permute-start = (bf16[2,128,256]{2,1,0:T(8,128)(2,1)S(1)}, bf16[2,128,256]{2,1,0:T(8,128)(2,1)S(1)}, u32[]{:S(2)}, u32[]{:S(2)}) collective-permute-start(bf16[2,128,256]{2,1,0:T(8,128)(2,1)S(1)} %slice_select_fusion), channel_id=1, source_target_pairs={{4,8},{12,16},{20,24},{28,32},{36,40},{44,48},{52,56},{60,64},{68,... | collective-permute-start | bytes 393224 | tf_op jit(solution)/shard_map/ppermute | solution.py:36
  37.4 23.4 %all-to-all-start.3 = ((bf16[4,16,768]{2,1,0:T(8,128)(2,1)}), bf16[4,16,768]{2,1,0:T(8,128)(2,1)S(1)}, u32[]{:S(2)}, u32[]{:S(2)}) async-start(bf16[4,16,768]{2,1,0:T(8,128)(2,1)} %broadcast_in_dim.24), calls=%async_computation.3 | async-start | bytes 196608 | tf_op jit(solution)/shard_map/all_to_all | solution.py:41
  61.4 8.2 %all-to-all-start.1 = ((f32[4,1,256]{2,1,0:T(1,128)}), f32[4,1,256]{2,1,0:T(1,128)S(1)}, u32[]{:S(2)}, u32[]{:S(2)}) async-start(f32[4,1,256]{2,1,0:T(1,128)} %broadcast_in_dim.23), calls=%async_computation.1 | async-start | bytes 8192 | tf_op jit(solution)/shard_map/all_to_all | solution.py:41
  70.3 15.0 %all-to-all-start.4 = ((bf16[16,16,768]{2,1,0:T(8,128)(2,1)}), bf16[16,16,768]{2,1,0:T(8,128)(2,1)S(1)}, u32[]{:S(2)}, u32[]{:S(2)}) async-start(bf16[16,16,768]{2,1,0:T(8,128)(2,1)} %broadcast_in_dim.25), calls=%async_computation.4 | async-start | bytes 786432 | tf_op jit(solution)/shard_map/all_to_all | solution.py:41
  103.7 0.7 copy-start.8
  104.2 0.7 copy-start.7
